TPU v7x, 256 devices: a whole 4x4x8 slice. The times are simulated.
256 devices in a mesh: side: 2 (over x_hi), row: 32 (over y, z), col: 4 (over x_lo, core).
Axes of the slice: x: 4 (x_hi: 2, x_lo: 2; x = x_hi * 2 + x_lo), y: 4, z: 8, core: 2. Of those that a mesh axis runs over, the one named last changes fastest.
Arguments:
- old_vectors: bfloat16 [2, 32768, 16384], P('side', 'row', 'col'), may hold values from -6 to 6
- reflectors: bfloat16 [2, 2, 32768, 512], P('side', None, 'row', 'col'), may hold values from -0.0625 to 0.0625
- triangles: float32 [2, 2, 512, 512], P('side'), may hold values from -0.25 to 0.25
- pole_sq: float32 [32768], replicated, may hold values from 1 to 65536, as said below
- coupling: float32 [32768], replicated, may hold values from -1 to 1
- deflated: int32 [32768], replicated, may hold values 0 or 1
- pole_order: int32 [32768], replicated, may hold values from 0 to 32767, each once
- anchors: int32 [1024], replicated, may hold values from 0 to 32766, as said below
- root_fraction: float32 [1024], replicated, may hold values from 0.2 to 0.8
Outputs:
- vectors: bfloat16 [2, 1024, 32768], P('side', 'col', 'row')
Inputs may be any that keep to these rules, and one draw needn't show every extreme that they name: `pole_sq`: strictly increasing; successive entries differ by 0.5 or more. `anchors`: distinct entries.
All inputs are finite; a program needn't handle non-finite values.
Results may differ from a plain program's by a relative error of at most 0.014.
Values may be sent and summed in bfloat16 or wider, within the bound.
A program may use at most 128 MiB of HBM per device.

v0:
```python
import jax
import jax.numpy as jnp
from jax import lax
from jax.sharding import PartitionSpec as P


def secular_columns(col_sq, col_coupling, col_live, weight, anchor_sq, pole_gap, root_fraction):
    denom = col_sq[:, None] - anchor_sq[None, :] - root_fraction[None, :] * pole_gap[None, :]
    return (col_live * col_coupling * weight)[:, None] / denom


def per_device(
    old_vectors,
    reflectors,
    triangles,
    pole_sq,
    coupling,
    deflated,
    pole_order,
    anchors,
    root_fraction,
):
    side_index = lax.axis_index("side")
    row_index = lax.axis_index("row")
    col_index = lax.axis_index("col")
    half_rows = lax.axis_size("row") // 2
    col_count = lax.axis_size("col")
    old_block = old_vectors[0]
    col_width = old_block.shape[1]
    order_size = pole_sq.shape[0]
    triplets = anchors.shape[0]
    local_triplets = triplets // col_count
    first_column = row_index // half_rows * (order_size // 2) + col_index * col_width
    columns = first_column + jnp.arange(col_width, dtype=jnp.int32)
    position = (
        jnp.zeros((order_size,), jnp.int32)
        .at[pole_order]
        .set(jnp.arange(order_size, dtype=jnp.int32))
    )
    sorted_pos = lax.dynamic_slice_in_dim(position, first_column, col_width)
    col_sq = pole_sq[sorted_pos]
    col_coupling = coupling[sorted_pos]
    col_live = (1 - deflated[sorted_pos]).astype(jnp.float32)
    weight = jnp.where(side_index == 0, jnp.ones_like(col_sq), jnp.sqrt(col_sq))
    anchor_sq = pole_sq[anchors]
    pole_gap = pole_sq[anchors + 1] - anchor_sq
    dead_triplet = deflated[anchors] == 1
    target = pole_order[anchors]
    secular = secular_columns(
        col_sq, col_coupling, col_live, weight, anchor_sq, pole_gap, root_fraction
    )
    onehot = (columns[:, None] == target[None, :]).astype(jnp.float32)
    mixing = jnp.where(dead_triplet[None, :], onehot, secular).astype(jnp.bfloat16)
    share_size = col_width // half_rows
    slice_part = lax.dynamic_slice_in_dim(
        secular, row_index % half_rows * share_size, share_size, 0
    )
    squares = lax.psum(jnp.sum(slice_part * slice_part, axis=0), ("row", "col"))
    col_scale = jnp.where(dead_triplet, jnp.ones_like(squares), 1.0 / jnp.sqrt(squares + 1e-06))
    merged = lax.psum_scatter(
        jnp.einsum("ck,rc->kr", mixing, old_block, preferred_element_type=jnp.float32).astype(
            jnp.bfloat16
        ),
        "col",
        scatter_dimension=0,
        tiled=True,
    ).astype(jnp.float32)
    my_scale = lax.dynamic_slice_in_dim(col_scale, col_index * local_triplets, local_triplets)
    vectors = merged * my_scale[:, None]
    panel_local = reflectors[0]
    panels = panel_local.shape[0]
    upper_tri = jnp.triu(triangles[0])
    highest = lax.Precision.HIGHEST
    for panel_index in reversed(range(panels)):
        panel_rows = panel_local[panel_index]
        current = vectors
        current_low = current.astype(jnp.bfloat16)
        projected = jnp.dot(
            current_low,
            lax.all_gather(panel_rows, "col", axis=1, tiled=True),
            preferred_element_type=jnp.float32,
        )
        projected = lax.psum(projected.astype(jnp.bfloat16), "row").astype(jnp.float32)
        coefficients = jnp.dot(projected, upper_tri[panel_index].T, precision=highest).astype(
            jnp.bfloat16
        )
        vectors = current - jnp.dot(
            coefficients,
            lax.all_gather(panel_rows, "col", axis=1, tiled=True).T,
            preferred_element_type=jnp.float32,
        )
    return vectors.astype(jnp.bfloat16)[None]


def solution(mesh):
    in_specs = (
        P("side", "row", "col"),
        P("side", None, "row", "col"),
        P("side", None, None, None),
        P(),
        P(),
        P(),
        P(),
        P(),
        P(),
    )
    out_specs = P("side", "col", "row")
    return jax.shard_map(
        per_device, mesh=mesh, in_specs=in_specs, out_specs=out_specs, check_vma=False
    )
```

profile of v0, /device:TPU:2, one launch (start us, length us, event | category | flops | bytes accessed | tf_op | source)
XLA Modules:
  0.0 883.1 jit_solution(16158088718118967877)
XLA Ops:
  6.5 0.0 copy-start
  6.5 0.0 all-gather.5.cloned.1.call-start
  6.5 1.9 fusion.23
  8.4 0.0 all-gather.5.cloned.1.call-update
  8.4 0.0 reduce-scatter.2.cloned.1.call-start
  8.5 0.9 compare_select_fusion
  9.5 120.1 %scatter_custom_fusion = s32[32768]{0:T(1024)S(1)} fusion(s32[32768]{0:T(1024)S(1)} %compare_select_fusion, s32[32768]{0:T(1024)S(1)} %iota.24, s32[]{:T(128)} %constant.23.clone.1), kind=kCustom, calls=%fused_computation.38 | custom fusion | bytes 131076 | tf_op jit(solution)/shard_map/scatter | solution.py:38
  129.6 0.0 copy-start.4
  129.6 0.0 copy-start.1
  129.6 19.5 %gather_fusion.2 = s32[4096]{0:T(1024)S(1)} fusion(s32[32768]{0:T(1024)} %param.14, s32[4096]{0:T(1024)S(1)} %fusion.20), kind=kCustom, calls=%fused_computation.2 | custom fusion | bytes 49152 | tf_op jit(solution)/shard_map/gather | solution.py:43
  149.2 0.0 copy-done
  149.2 0.0 copy-start.3
  149.2 0.0 copy-start.2
  149.2 23.0 %gather_fusion.4 = f32[4096]{0:T(1024)S(1)} fusion(f32[32768]{0:T(1024)S(1)} %copy-done, s32[4096]{0:T(1024)S(1)} %fusion.20), kind=kCustom, calls=%fused_computation.4 | custom fusion | bytes 49152 | tf_op jit(solution)/shard_map/gather | solution.py:41
  172.2 0.0 copy-done.4
  172.3 0.0 copy-start.5
  172.3 6.2 gather_fusion.5
  178.4 0.0 copy-done.1
  178.4 6.2 gather_fusion
  184.6 0.0 copy-done.3
  184.6 6.2 gather_fusion.1
  190.8 0.0 copy-done.2
  190.8 23.0 %gather_fusion.3 = f32[4096]{0:T(1024)S(1)} fusion(f32[32768]{0:T(1024)S(1)} %copy-done.2, s32[4096]{0:T(1024)S(1)} %fusion.20), kind=kCustom, calls=%fused_computation.3 | custom fusion | bytes 49152 | tf_op jit(solution)/shard_map/gather | solution.py:42
  213.8 6.2 gather_fusion.6
  220.0 6.5 subtract_divide_fusion
  226.5 1.3 multiply_reduce_fusion
  227.8 278.5 %psum.21 = f32[1024]{0:T(1024)S(1)} all-reduce(f32[1024]{0:T(1024)S(1)} %multiply_reduce_fusion), channel_id=1, replica_groups=mesh['side'=2,'row'=32,'col'=4] {'row','col'}, use_global_device_ids=true, to_apply=%region_3.4 | all-reduce | flops 1024 | bytes 8192 | tf_op jit(solution)/shard_map/psum | solution.py:58
  506.3 15.3 %fusion.5 = bf16[1024,1024]{1,0:T(8,128)(2,1)} fusion(bf16[1,1024,4096]{2,1,0:T(8,128)(2,1)} %param.9, s32[1024]{0:T(1024)S(1)} %gather_fusion.1, s32[4096]{0:T(1024)S(1)} %iota_add_fusion, pred[1024]{0:T(1024)(128)(4,1)S(1)} %get-tuple-element.6, f32[1024]{0:T(1024)S(1)} %subtract_multiply_fusion, f32[1024]{0:T(1024)S(1)} %gather_fusion.5, ...), kind=kOutput, calls=%fused_computation.16 | convolution fusion | flops 8620343296 | bytes 10548224 | tf_op jit(solution)/shard_map/ck,rc->kr/dot_general | solution.py:61
  521.7 0.0 reduce-scatter.2.cloned.1.call-update
  521.7 0.0 all-reduce.3.cloned.1.call-start
  521.8 0.1 dynamic_slice.11
  521.8 28.4 %reduce-scatter.2.cloned.1.call-done = bf16[256,1024]{1,0:T(8,128)(2,1)} async-done(((bf16[1024,1024]{1,0:T(8,128)(2,1)}), bf16[256,1024]{1,0:T(8,128)(2,1)}) %reduce-scatter.2.cloned.1.call-update) | async-done | bytes 524304 | tf_op jit(solution)/shard_map/reduce_scatter | solution.py:60
  550.3 2.6 convolution_convert_fusion.3
  552.9 0.0 all-reduce.3.cloned.1.call-update
  552.9 0.0 all-gather.7.cloned.1.call-start
  552.9 0.5 all-gather.7.cloned.1.call-update
  553.5 0.3 all-reduce.5.cloned.1.call-start
  553.7 0.2 iota_compare_fusion
  554.0 2.0 bitcast_select_fusion
  555.9 145.1 %all-reduce.3.cloned.1.call-done = bf16[256,512]{1,0:T(8,128)(2,1)} async-done(((bf16[256,512]{1,0:T(8,128)(2,1)}), bf16[256,512]{1,0:T(8,128)(2,1)}) %all-reduce.3.cloned.1.call-update) | async-done | bytes 262160 | tf_op jit(solution)/shard_map/psum | solution.py:83
  701.0 1.6 convolution_convert_fusion.2
  702.6 1.8 convolution_subtract_fusion.1
  704.5 18.7 %all-gather.7.cloned.1.call-done = bf16[1,1,1024,512]{3,2,1,0:T(8,128)(2,1)} async-done(((bf16[1,1,1024,128]{3,2,1,0:T(8,128)(2,1)}), bf16[1,1,1024,512]{3,2,1,0:T(8,128)(2,1)}) %all-gather.7.cloned.1.call-update) | async-done | bytes 1048592 | tf_op jit(solution)/shard_map/all_gather | solution.py:80
  723.1 2.4 convolution_convert_fusion.1
  725.5 0.0 all-reduce.5.cloned.1.call-update
  725.5 146.9 %all-reduce.5.cloned.1.call-done = bf16[256,512]{1,0:T(8,128)(2,1)} async-done(((bf16[256,512]{1,0:T(8,128)(2,1)}), bf16[256,512]{1,0:T(8,128)(2,1)}) %all-reduce.5.cloned.1.call-update) | async-done | bytes 262160 | tf_op jit(solution)/shard_map/psum | solution.py:83
  872.4 1.6 convolution_convert_fusion
  874.1 2.5 fusion.9
  (10 shorter events, 0.1 us)
Async XLA Ops:
  6.5 142.6 %copy-start = (f32[32768]{0:T(1024)S(1)}, f32[32768]{0:T(1024)}, u32[]{:S(2)}) copy-start(f32[32768]{0:T(1024)} %param.12) | copy-start | bytes 393220
  6.5 515.3 %all-gather.5.cloned.1.call-start = ((), (), s32[]{:S(2)}) async-start(), calls=%async_computation.4 | async-start | bytes 1310720 | tf_op jit(solution)/shard_map/all_gather | solution.py:80
  8.4 541.8 %reduce-scatter.2.cloned.1.call-start = ((), (), s32[]{:S(2)}) async-start(), calls=%async_computation.1 | async-start | bytes 2621440 | tf_op jit(solution)/shard_map/reduce_scatter | solution.py:60
  129.6 42.6 %copy-start.4 = (s32[1024]{0:T(1024)S(1)}, s32[1024]{0:T(1024)}, u32[]{:S(2)}) copy-start(s32[1024]{0:T(1024)} %param.16) | copy-start | bytes 12292
  129.6 48.8 %copy-start.1 = (s32[32768]{0:T(1024)S(1)}, s32[32768]{0:T(1024)}, u32[]{:S(2)}) copy-start(s32[32768]{0:T(1024)} %param.14) | copy-start | bytes 393220
  149.2 35.4 %copy-start.3 = (s32[32768]{0:T(1024)S(1)}, s32[32768]{0:T(1024)}, u32[]{:S(2)}) copy-start(s32[32768]{0:T(1024)} %param.15) | copy-start | bytes 393220
  149.2 41.6 %copy-start.2 = (f32[32768]{0:T(1024)S(1)}, f32[32768]{0:T(1024)}, u32[]{:S(2)}) copy-start(f32[32768]{0:T(1024)} %param.13) | copy-start | bytes 393220
  172.3 47.7 %copy-start.5 = (f32[1024]{0:T(1024)S(1)}, f32[1024]{0:T(1024)}, u32[]{:S(2)}) copy-start(f32[1024]{0:T(1024)} %param.17) | copy-start | bytes 12292
  521.7 179.3 %all-reduce.3.cloned.1.call-start = ((), (), s32[]{:S(2)}) async-start(), calls=%async_computation.2 | async-start | bytes 524288 | tf_op jit(solution)/shard_map/psum | solution.py:83
  552.9 170.3 %all-gather.7.cloned.1.call-start = ((), (), s32[]{:S(2)}) async-start(), calls=%async_computation.5 | async-start | bytes 1310720 | tf_op jit(solution)/shard_map/all_gather | solution.py:80
  553.5 319.0 %all-reduce.5.cloned.1.call-start = ((), (), s32[]{:S(2)}) async-start(), calls=%async_computation.3 | async-start | bytes 524288 | tf_op jit(solution)/shard_map/psum | solution.py:83
Sparse Core Ops, SparseCore 0:
  9.2 26.2 all-gather.4
  521.8 28.4 reduce-scatter.1
  554.1 146.8 all-reduce.2
  702.8 20.2 all-gather.6
  726.8 145.5 all-reduce.4
where the time goes:
time: 884 us; the launch traced here: 883 us
  waiting for transfers between devices  340 us (38%)
  blocking collectives  278 us (31%)
  local copies, waits for them, and re-layouts  212 us (24%)
  matrix products  27.8 us (3%)
  between operations  13.4 us (2%)
  other arithmetic  10.9 us (1%)
    psum x2, waiting for transfers between devices, per_device(): lax.psum(projected.astype(jnp.bfloat16), 'row').astype(jnp.float32)  292 us
    psum x1, blocking collectives, per_device(): squares = lax.psum(jnp.sum(slice_part * slice_part, axis=0), ('row', 'col'))  278 us
    scatter x1, local copies, waits for them, and re-layouts, per_device(): position = jnp.zeros((order_size,), jnp.int32).at[pole_order].set(jnp.ara...  120 us
    reduce_scatter x1, waiting for transfers between devices, per_device(): lax.psum_scatter(jnp.einsum('ck,rc->kr', mixing, old_block, preferred_ele...  28.4 us
    gather x1, local copies, waits for them, and re-layouts, per_device(): col_sq = pole_sq[sorted_pos]  23 us
    gather x1, local copies, waits for them, and re-layouts, per_device(): col_coupling = coupling[sorted_pos]  23 us
    gather x1, local copies, waits for them, and re-layouts, per_device(): col_live = (1 - deflated[sorted_pos]).astype(jnp.float32)  19.5 us
    all_gather x2, waiting for transfers between devices, per_device(): lax.all_gather(panel_rows, 'col', axis=1, tiled=True)  18.7 us
  transfers between devices with their start and end apart: 5, of which 4 were waited for; matrix products, arithmetic and copies ran while one was open for 27% of the time, Pallas kernels for 0%

commit v1 on v0

--- a/solution.py
+++ b/solution.py
@@ -55,7 +55,7 @@
     slice_part = lax.dynamic_slice_in_dim(
         secular, row_index % half_rows * share_size, share_size, 0
     )
-    squares = lax.psum(jnp.sum(slice_part * slice_part, axis=0), ("row", "col"))
+    squares = lax.psum(lax.psum(jnp.sum(slice_part * slice_part, axis=0), "col"), "row")
     col_scale = jnp.where(dead_triplet, jnp.ones_like(squares), 1.0 / jnp.sqrt(squares + 1e-06))
     merged = lax.psum_scatter(
         jnp.einsum("ck,rc->kr", mixing, old_block, preferred_element_type=jnp.float32).astype(

time: 884 us -> 684 us (0.77)
  blocking collectives: 278 us -> 84 us
    psum x1 -> x2, blocking collectives: 278 us -> 84 us  [the longest x1 78.2 us: per_device(): lax.psum(lax.psum(jnp.sum(slice_part * slice_part, axis=0), 'col'), 'row')]
  transfers between devices with their start and end apart: 5 -> 5, of which waited for: 4 -> 4; matrix products, arithmetic and copies ran while one was open for 27% -> 35% of each run, Pallas kernels for 0% -> 0%
where the time goes in v1:
time: 684 us
  waiting for transfers between devices  335 us (49%)
  local copies, waits for them, and re-layouts  212 us (31%)
  blocking collectives  84 us (12%)
  matrix products  27.8 us (4%)
  between operations  13.4 us (2%)
  other arithmetic  10.9 us (2%)
    psum x2, waiting for transfers between devices, per_device(): lax.psum(projected.astype(jnp.bfloat16), 'row').astype(jnp.float32)  292 us
    scatter x1, local copies, waits for them, and re-layouts, per_device(): position = jnp.zeros((order_size,), jnp.int32).at[pole_order].set(jnp.ara...  120 us
    psum x1, blocking collectives, per_device(): lax.psum(lax.psum(jnp.sum(slice_part * slice_part, axis=0), 'col'), 'row')  78.2 us
    reduce_scatter x1, waiting for transfers between devices, per_device(): lax.psum_scatter(jnp.einsum('ck,rc->kr', mixing, old_block, preferred_ele...  23.5 us
    gather x1, local copies, waits for them, and re-layouts, per_device(): col_sq = pole_sq[sorted_pos]  23 us
    gather x1, local copies, waits for them, and re-layouts, per_device(): col_coupling = coupling[sorted_pos]  23 us
    gather x1, local copies, waits for them, and re-layouts, per_device(): col_live = (1 - deflated[sorted_pos]).astype(jnp.float32)  19.5 us
    all_gather x2, waiting for transfers between devices, per_device(): lax.all_gather(panel_rows, 'col', axis=1, tiled=True)  18.7 us
  transfers between devices with their start and end apart: 5, of which 4 were waited for; matrix products, arithmetic and copies ran while one was open for 35% of the time, Pallas kernels for 0%

profile of v1, /device:TPU:2, one launch (start us, length us, event | category | flops | bytes accessed | tf_op | source)
XLA Modules:
  0.0 683.6 jit_solution(9595648558337570840)
XLA Ops:
  6.5 0.0 copy-start
  6.5 0.0 all-gather.5.cloned.1.call-start
  6.5 1.9 fusion.23
  8.4 0.0 all-gather.5.cloned.1.call-update
  8.4 0.0 reduce-scatter.2.cloned.1.call-start
  8.5 0.9 compare_select_fusion
  9.5 120.1 %scatter_custom_fusion = s32[32768]{0:T(1024)S(1)} fusion(s32[32768]{0:T(1024)S(1)} %compare_select_fusion, s32[32768]{0:T(1024)S(1)} %iota.24, s32[]{:T(128)} %constant.23.clone.1), kind=kCustom, calls=%fused_computation.38 | custom fusion | bytes 131076 | tf_op jit(solution)/shard_map/scatter | solution.py:38
  129.6 0.0 copy-start.4
  129.6 0.0 copy-start.1
  129.6 19.5 %gather_fusion.2 = s32[4096]{0:T(1024)S(1)} fusion(s32[32768]{0:T(1024)} %param.14, s32[4096]{0:T(1024)S(1)} %fusion.20), kind=kCustom, calls=%fused_computation.2 | custom fusion | bytes 49152 | tf_op jit(solution)/shard_map/gather | solution.py:43
  149.2 0.0 copy-done
  149.2 0.0 copy-start.3
  149.2 0.0 copy-start.2
  149.2 23.0 %gather_fusion.4 = f32[4096]{0:T(1024)S(1)} fusion(f32[32768]{0:T(1024)S(1)} %copy-done, s32[4096]{0:T(1024)S(1)} %fusion.20), kind=kCustom, calls=%fused_computation.4 | custom fusion | bytes 49152 | tf_op jit(solution)/shard_map/gather | solution.py:41
  172.2 0.0 copy-done.4
  172.3 0.0 copy-start.5
  172.3 6.2 gather_fusion.5
  178.4 0.0 copy-done.1
  178.4 6.2 gather_fusion
  184.6 0.0 copy-done.3
  184.6 6.2 gather_fusion.1
  190.8 23.0 %gather_fusion.3 = f32[4096]{0:T(1024)S(1)} fusion(f32[32768]{0:T(1024)S(1)} %copy-done.2, s32[4096]{0:T(1024)S(1)} %fusion.20), kind=kCustom, calls=%fused_computation.3 | custom fusion | bytes 49152 | tf_op jit(solution)/shard_map/gather | solution.py:42
  213.8 6.2 gather_fusion.6
  220.0 6.4 subtract_divide_fusion
  226.5 1.3 multiply_reduce_fusion
  227.8 5.8 psum.28
  233.6 78.2 %psum.29 = f32[1024]{0:T(1024)S(1)} all-reduce(f32[1024]{0:T(1024)S(1)} %psum.28), channel_id=1, replica_groups=mesh['side'=2,'row'=32,'col'=4] {'row'}, use_global_device_ids=true, to_apply=%region_4.5 | all-reduce | flops 1024 | bytes 8192 | tf_op jit(solution)/shard_map/psum | solution.py:58
  311.8 15.3 %fusion.5 = bf16[1024,1024]{1,0:T(8,128)(2,1)} fusion(bf16[1,1024,4096]{2,1,0:T(8,128)(2,1)} %param.9, s32[1024]{0:T(1024)S(1)} %gather_fusion.1, s32[4096]{0:T(1024)S(1)} %iota_add_fusion, pred[1024]{0:T(1024)(128)(4,1)S(1)} %get-tuple-element.6, f32[1024]{0:T(1024)S(1)} %subtract_multiply_fusion, f32[1024]{0:T(1024)S(1)} %gather_fusion.5, ...), kind=kOutput, calls=%fused_computation.16 | convolution fusion | flops 8620343296 | bytes 10548224 | tf_op jit(solution)/shard_map/ck,rc->kr/dot_general | solution.py:61
  327.1 0.0 reduce-scatter.2.cloned.1.call-update
  327.2 0.0 all-reduce.3.cloned.1.call-start
  327.2 0.1 dynamic_slice.11
  327.3 23.5 %reduce-scatter.2.cloned.1.call-done = bf16[256,1024]{1,0:T(8,128)(2,1)} async-done(((bf16[1024,1024]{1,0:T(8,128)(2,1)}), bf16[256,1024]{1,0:T(8,128)(2,1)}) %reduce-scatter.2.cloned.1.call-update) | async-done | bytes 524304 | tf_op jit(solution)/shard_map/reduce_scatter | solution.py:60
  350.8 2.6 convolution_convert_fusion.3
  353.4 0.0 all-reduce.3.cloned.1.call-update
  353.4 0.0 all-gather.7.cloned.1.call-start
  353.5 0.5 all-gather.7.cloned.1.call-update
  354.0 0.3 all-reduce.5.cloned.1.call-start
  354.3 0.2 iota_compare_fusion
  354.5 2.0 bitcast_select_fusion
  356.4 145.1 %all-reduce.3.cloned.1.call-done = bf16[256,512]{1,0:T(8,128)(2,1)} async-done(((bf16[256,512]{1,0:T(8,128)(2,1)}), bf16[256,512]{1,0:T(8,128)(2,1)}) %all-reduce.3.cloned.1.call-update) | async-done | bytes 262160 | tf_op jit(solution)/shard_map/psum | solution.py:83
  501.6 1.6 convolution_convert_fusion.2
  503.2 1.8 convolution_subtract_fusion.1
  505.0 18.7 %all-gather.7.cloned.1.call-done = bf16[1,1,1024,512]{3,2,1,0:T(8,128)(2,1)} async-done(((bf16[1,1,1024,128]{3,2,1,0:T(8,128)(2,1)}), bf16[1,1,1024,512]{3,2,1,0:T(8,128)(2,1)}) %all-gather.7.cloned.1.call-update) | async-done | bytes 1048592 | tf_op jit(solution)/shard_map/all_gather | solution.py:80
  523.7 2.4 convolution_convert_fusion.1
  526.1 0.0 all-reduce.5.cloned.1.call-update
  526.1 146.9 %all-reduce.5.cloned.1.call-done = bf16[256,512]{1,0:T(8,128)(2,1)} async-done(((bf16[256,512]{1,0:T(8,128)(2,1)}), bf16[256,512]{1,0:T(8,128)(2,1)}) %all-reduce.5.cloned.1.call-update) | async-done | bytes 262160 | tf_op jit(solution)/shard_map/psum | solution.py:83
  673.0 1.6 convolution_convert_fusion
  674.6 2.5 fusion.9
  (11 shorter events, 0.1 us)
Async XLA Ops:
  6.5 142.6 %copy-start = (f32[32768]{0:T(1024)S(1)}, f32[32768]{0:T(1024)}, u32[]{:S(2)}) copy-start(f32[32768]{0:T(1024)} %param.12) | copy-start | bytes 393220
  6.5 320.8 %all-gather.5.cloned.1.call-start = ((), (), s32[]{:S(2)}) async-start(), calls=%async_computation.4 | async-start | bytes 1310720 | tf_op jit(solution)/shard_map/all_gather | solution.py:80
  8.4 342.3 %reduce-scatter.2.cloned.1.call-start = ((), (), s32[]{:S(2)}) async-start(), calls=%async_computation.1 | async-start | bytes 2621440 | tf_op jit(solution)/shard_map/reduce_scatter | solution.py:60
  129.6 42.6 %copy-start.4 = (s32[1024]{0:T(1024)S(1)}, s32[1024]{0:T(1024)}, u32[]{:S(2)}) copy-start(s32[1024]{0:T(1024)} %param.16) | copy-start | bytes 12292
  129.6 48.8 %copy-start.1 = (s32[32768]{0:T(1024)S(1)}, s32[32768]{0:T(1024)}, u32[]{:S(2)}) copy-start(s32[32768]{0:T(1024)} %param.14) | copy-start | bytes 393220
  149.2 35.4 %copy-start.3 = (s32[32768]{0:T(1024)S(1)}, s32[32768]{0:T(1024)}, u32[]{:S(2)}) copy-start(s32[32768]{0:T(1024)} %param.15) | copy-start | bytes 393220
  149.2 41.6 %copy-start.2 = (f32[32768]{0:T(1024)S(1)}, f32[32768]{0:T(1024)}, u32[]{:S(2)}) copy-start(f32[32768]{0:T(1024)} %param.13) | copy-start | bytes 393220
  172.3 47.7 %copy-start.5 = (f32[1024]{0:T(1024)S(1)}, f32[1024]{0:T(1024)}, u32[]{:S(2)}) copy-start(f32[1024]{0:T(1024)} %param.17) | copy-start | bytes 12292
  327.2 174.4 %all-reduce.3.cloned.1.call-start = ((), (), s32[]{:S(2)}) async-start(), calls=%async_computation.2 | async-start | bytes 524288 | tf_op jit(solution)/shard_map/psum | solution.py:83
  353.4 170.3 %all-gather.7.cloned.1.call-start = ((), (), s32[]{:S(2)}) async-start(), calls=%async_computation.5 | async-start | bytes 1310720 | tf_op jit(solution)/shard_map/all_gather | solution.py:80
  354.0 319.0 %all-reduce.5.cloned.1.call-start = ((), (), s32[]{:S(2)}) async-start(), calls=%async_computation.3 | async-start | bytes 524288 | tf_op jit(solution)/shard_map/psum | solution.py:83
Sparse Core Ops, SparseCore 0:
  9.2 26.2 all-gather.4
  327.3 23.4 reduce-scatter.1
  354.7 146.8 all-reduce.2
  503.4 20.2 all-gather.6
  527.4 145.5 all-reduce.4
